TPU v7x, 32 devices: a whole 2x2x4 slice. The times are simulated.
32 devices in a mesh: depth: 4 (over x, core), map: 8 (over z, y).
Axes of the slice: x: 2, y: 2, z: 4, core: 2. Of those that a mesh axis runs over, the one named last changes fastest.
Arguments:
- adjoint: float32 [35, 9, 16384], P(None, None, ('depth', 'map')), may hold values from -6 to 6
- forward: bfloat16 [2, 35, 9, 16384], P(None, None, None, ('depth', 'map')), may hold values from -6 to 6
- p_speed: float32 [16384], P(('depth', 'map')), may hold values from 1.5 to 2.5
- s_speed: float32 [16384], P(('depth', 'map')), may hold values from 0.5 to 1
- density: float32 [16384], P(('depth', 'map')), may hold values from 0.8 to 1.6
- inv_jacobian: float32 [3, 3, 16384], P(None, None, ('depth', 'map')), may hold values from -1 to 1
- face_angles: float32 [2, 4, 16384], P(None, None, ('depth', 'map')), may hold values from -3.140625 to 3.140625
- face_scale: float32 [4, 16384], P(None, ('depth', 'map')), may hold values from 0.25 to 1
- stiffness: float32 [3, 35, 35], replicated, may hold values from -1 to 1
- face_basis: float32 [4, 35, 15], replicated, may hold values from -1 to 1
- neighbours: int32 [4, 16384], P(None, ('depth', 'map')), may hold values from 0 to 768, as said below
- neighbour_face: int32 [4, 16384], P(None, ('depth', 'map')), may hold values from 0 to 3
- send_elements: int32 [4, 2048], P(None, ('depth', 'map')), may hold values from 0 to 511
- send_faces: int32 [4, 2048], P(None, ('depth', 'map')), may hold values from 0 to 3
- cell_index: int32 [16384], P(('depth', 'map')), may hold values from 0 to 511, as said below
Outputs:
- adjoint_out: float32 [35, 9, 16384], P(None, None, ('depth', 'map'))
- kernels: float32 [3, 512], P(None, ('depth', 'map'))
Inputs may be any that keep to these rules, and one draw needn't show every extreme that they name: `neighbours`: entries below 512 name a local element of the same device; 512 + r * 64 + k names entry k of ghost slot r; 768 marks a boundary face. `cell_index`: local element k of device d lies in coarse cell s = d * 16 + k // 32 or in one next to it (s - 1 or s + 1, within 0 to 511); coarse cells are owned cyclically, so the entry is (s mod the number of devices) * 16 + s // the number of devices.
All inputs are finite; a program needn't handle non-finite values.
Results may differ from a plain program's by a relative error of at most 0.0003.
Values sent between devices are 32-bit elements; how exact they have to be, the bound alone decides.
A program may use at most 192 MiB of HBM per device.

v0:
```python
import jax
import jax.numpy as jnp
from jax import lax
from jax.sharding import PartitionSpec as P

PICARD = 4


HIGH = lax.Precision.HIGHEST
TIME_STEP = 0.3
KERNEL_WEIGHT = 0.125


def shifted(value, axis, steps):
    count = lax.axis_size(axis)
    initial, last = (max(0, -steps), min(count, count - steps))
    return lax.ppermute(value, axis, [(source, source + steps) for source in range(initial, last)])


def star_apply(normal, coeffs, field):
    lame_first, shear_mod, inverse_density = coeffs
    along_x, along_y, along_z = (normal[0], normal[1], normal[2])
    long_mod = lame_first + 2.0 * shear_mod
    velocity_x, velocity_y, velocity_z = (field[:, 6], field[:, 7], field[:, 8])
    rows = [
        -(
            long_mod * along_x * velocity_x
            + lame_first * along_y * velocity_y
            + lame_first * along_z * velocity_z
        ),
        -(
            lame_first * along_x * velocity_x
            + long_mod * along_y * velocity_y
            + lame_first * along_z * velocity_z
        ),
        -(
            lame_first * along_x * velocity_x
            + lame_first * along_y * velocity_y
            + long_mod * along_z * velocity_z
        ),
        -shear_mod * (along_y * velocity_x + along_x * velocity_y),
        -shear_mod * (along_z * velocity_y + along_y * velocity_z),
        -shear_mod * (along_z * velocity_x + along_x * velocity_z),
        -inverse_density * (along_x * field[:, 0] + along_y * field[:, 3] + along_z * field[:, 5]),
        -inverse_density * (along_x * field[:, 3] + along_y * field[:, 1] + along_z * field[:, 4]),
        -inverse_density * (along_x * field[:, 5] + along_y * field[:, 4] + along_z * field[:, 2]),
    ]
    return jnp.stack(rows, axis=1)


def material(p_speed, s_speed, density):
    lame_first = density * (p_speed * p_speed - 2.0 * s_speed * s_speed)
    shear_mod = density * s_speed * s_speed
    return (lame_first, shear_mod, 1.0 / density)


def normal_vectors(face_angles):
    azimuth, polar = (face_angles[0], face_angles[1])
    return jnp.stack(
        [jnp.cos(azimuth) * jnp.sin(polar), jnp.sin(azimuth) * jnp.sin(polar), jnp.cos(polar)],
        axis=0,
    )


def volume_term(dofs, inv_jacobian, coeffs, stiffness):
    basis, fields, count = dofs.shape
    flat = dofs.reshape(basis, fields * count)
    total = jnp.zeros(dofs.shape, jnp.float32)
    for coord in range(3):
        moved = jnp.dot(stiffness[coord].T, flat, precision=HIGH).reshape(basis, fields, count)
        total = total + star_apply(inv_jacobian[coord], coeffs, moved)
    return total


def predict(dofs, inv_jacobian, coeffs, stiffness, sweeps):
    current = dofs
    for sweep in range(sweeps):
        current = dofs + 0.5 * TIME_STEP * volume_term(current, inv_jacobian, coeffs, stiffness)
    return TIME_STEP * current


def one_face(flat, face_basis, face, fields, width):
    return jnp.dot(face_basis[face].T, flat, precision=HIGH).reshape(
        face_basis.shape[2], fields, width
    )


def all_face_traces(table, face_basis):
    basis, fields, width = table.shape
    flat = table.reshape(basis, fields * width)
    return jnp.concatenate(
        [one_face(flat, face_basis, face, fields, width) for face in range(4)], axis=2
    )


def apply_faces(
    update, traces, flat_index, inside, own_width, coeffs, p_speed, normals, face_scale, face_basis
):
    basis, fields, count = update.shape
    modes = face_basis.shape[2]
    for face in range(4):
        own = traces[:, :, face * own_width : face * own_width + count]
        far = jnp.take(traces, flat_index[face], axis=2) * inside[face].astype(jnp.float32)
        flux = 0.5 * star_apply(normals[:, face], coeffs, own + far) + 0.5 * p_speed * (own - far)
        flux = flux * face_scale[face]
        lifted = jnp.dot(face_basis[face], flux.reshape(modes, fields * count), precision=HIGH)
        update = update - lifted.reshape(basis, fields, count)
    return update


def element_kernels(integ, snapshot, p_speed, s_speed, density):
    forward_field = snapshot.astype(jnp.float32)
    product = integ * forward_field
    trace_adjoint = integ[:, 0] + integ[:, 1] + integ[:, 2]
    trace_forward = forward_field[:, 0] + forward_field[:, 1] + forward_field[:, 2]
    first = jnp.sum(trace_adjoint * trace_forward, axis=0)
    second = jnp.sum(
        product[:, 0]
        + product[:, 1]
        + product[:, 2]
        + 2.0 * (product[:, 3] + product[:, 4] + product[:, 5]),
        axis=0,
    )
    third = jnp.sum(product[:, 6] + product[:, 7] + product[:, 8], axis=0)
    speed_kernel = 2.0 * density * p_speed * first
    shear_kernel = density * s_speed * (2.0 * second - 4.0 * first)
    mass_kernel = (
        (p_speed * p_speed - 2.0 * s_speed * s_speed) * first + s_speed * s_speed * second + third
    )
    return KERNEL_WEIGHT * jnp.stack([speed_kernel, shear_kernel, mass_kernel], axis=1)


def depth_ids(faces, offset):
    return shifted(faces, "depth", offset)


def map_ids(faces, offset):
    return shifted(faces, "map", offset)


def depth_block(block, offset):
    return shifted(block, "depth", offset)


def map_block(block, offset):
    return shifted(block, "map", offset)


def shards(
    adjoint,
    forward,
    p_speed,
    s_speed,
    density,
    inv_jacobian,
    face_angles,
    face_scale,
    stiffness,
    face_basis,
    neighbours,
    neighbour_face,
    send_elements,
    send_faces,
    cell_index,
):
    coeffs = material(p_speed, s_speed, density)
    normals = normal_vectors(face_angles)
    count = adjoint.shape[2]
    ghost_total = 4 * send_elements.shape[1]
    total_cells = count // 32 * lax.axis_size("depth") * lax.axis_size("map")
    steps_total = forward.shape[0]
    state = adjoint
    kernels = jnp.zeros((3, count // 32), jnp.float32)
    limit = count + ghost_total
    inside = neighbours < limit
    safe = jnp.minimum(neighbours, limit - 1)
    ghost_faces = jnp.concatenate(
        [
            depth_ids(send_faces[0], 1),
            depth_ids(send_faces[1], -1),
            map_ids(send_faces[2], 1),
            map_ids(send_faces[3], -1),
        ],
        axis=0,
    )
    ghost_slot = jnp.clip(safe - count, 0, ghost_total - 1)
    far_face = jnp.where(safe < count, neighbour_face, ghost_faces[ghost_slot])
    flat_index = far_face * limit + safe
    for step in range(steps_total):
        integ = predict(state, inv_jacobian, coeffs, stiffness, PICARD)
        update = state + volume_term(integ, inv_jacobian, coeffs, stiffness)
        blocks = [jnp.take(integ, send_elements[slot], axis=2) for slot in range(4)]
        ghosts = jnp.concatenate(
            [
                depth_block(blocks[0], 1),
                depth_block(blocks[1], -1),
                map_block(blocks[2], 1),
                map_block(blocks[3], -1),
            ],
            axis=2,
        )
        table = jnp.concatenate([integ, ghosts], axis=2)
        traces = all_face_traces(table, face_basis)
        state = apply_faces(
            update,
            traces,
            flat_index,
            inside,
            limit,
            coeffs,
            p_speed,
            normals,
            face_scale,
            face_basis,
        )
        terms = element_kernels(integ, forward[step], p_speed, s_speed, density)
        step_hist = jax.ops.segment_sum(terms, cell_index, num_segments=total_cells).T
        kernels = kernels + lax.psum_scatter(
            step_hist, ("depth", "map"), scatter_dimension=1, tiled=True
        )
    return (state, kernels)


def solution(mesh):
    placed = (
        P(None, None, ("depth", "map")),
        P(None, None, None, ("depth", "map")),
        P(("depth", "map")),
        P(("depth", "map")),
        P(("depth", "map")),
        P(None, None, ("depth", "map")),
        P(None, None, ("depth", "map")),
        P(None, ("depth", "map")),
        P(),
        P(),
        P(None, ("depth", "map")),
        P(None, ("depth", "map")),
        P(None, ("depth", "map")),
        P(None, ("depth", "map")),
        P(("depth", "map")),
    )
    return jax.shard_map(
        shards,
        mesh=mesh,
        in_specs=placed,
        out_specs=(P(None, None, ("depth", "map")), P(None, ("depth", "map"))),
        check_vma=False,
    )
```

profile of v0, /device:TPU:0, one launch (start us, length us, event | category | flops | bytes accessed | tf_op | source)
XLA Modules:
  0.0 818.5 jit_solution(153735395530779889)
XLA Ops:
  14.1 5.4 collective-permute-start.6
  86.0 9.6 %copy-start.152 = (f32[512]{0:T(512)S(1)}, f32[512]{0:T(512)}, u32[]{:S(2)}) copy-start(f32[512]{0:T(512)} %copy-done.150) | copy-start | bytes 6148
  196.4 13.1 %gather_fusion = s32[2048]{0:T(1024)S(1)} fusion(s32[256]{0:T(256)S(1)} %pad_add_fusion, s32[2048]{0:T(1024)S(1)} %broadcast_clamp_fusion), kind=kCustom, calls=%fused_computation.16 | custom fusion | bytes 24576 | tf_op jit(solution)/shard_map/gather | solution.py:187
  224.8 5.9 copy.2031
  235.6 5.0 copy.2032
  240.6 5.0 copy.2033
  245.6 23.7 %pad_maximum_fusion = f32[15,9,3072]{1,0,2:T(8,128)} fusion(f32[15,9,768]{1,0,2:T(8,128)} %copy.2033, f32[15,9,768]{1,0,2:T(8,128)} %copy.2032, f32[15,9,768]{1,0,2:T(8,128)} %copy.2031, f32[15,9,768]{1,0,2:T(8,128)} %copy.2030), kind=kLoop, calls=%fused_computation.19 | loop fusion | flops 1244160 | bytes 3317760 | tf_op jit(solution)/shard_map/concatenate | solution.py:91
  269.3 11.1 %gather_fusion.8 = f32[512,15,9]{2,1,0:T(8,128)} fusion(f32[15,9,3072]{1,0,2:T(8,128)} %pad_maximum_fusion, s32[1024]{0:T(1024)S(1)} %get-tuple-element.579), kind=kCustom, calls=%fused_computation.11.clone | custom fusion | bytes 555008 | tf_op jit(solution)/shard_map/jit(_take)/gather | solution.py:103
  287.5 11.1 %gather_fusion.7 = f32[512,15,9]{2,1,0:T(8,128)} fusion(f32[15,9,3072]{1,0,2:T(8,128)} %pad_maximum_fusion, s32[1024]{0:T(1024)S(1)} %get-tuple-element.580), kind=kCustom, calls=%fused_computation.10.clone | custom fusion | bytes 555008 | tf_op jit(solution)/shard_map/jit(_take)/gather | solution.py:103
  305.7 11.1 %gather_fusion.6 = f32[512,15,9]{2,1,0:T(8,128)} fusion(f32[15,9,3072]{1,0,2:T(8,128)} %pad_maximum_fusion, s32[1024]{0:T(1024)S(1)} %get-tuple-element.581), kind=kCustom, calls=%fused_computation.9.clone | custom fusion | bytes 555008 | tf_op jit(solution)/shard_map/jit(_take)/gather | solution.py:103
  316.8 11.1 %gather_fusion.5 = f32[512,15,9]{2,1,0:T(8,128)} fusion(f32[15,9,3072]{1,0,2:T(8,128)} %pad_maximum_fusion, s32[1024]{0:T(1024)S(1)} %get-tuple-element.582), kind=kCustom, calls=%fused_computation.1.clone | custom fusion | bytes 555008 | tf_op jit(solution)/shard_map/jit(_take)/gather | solution.py:103
  461.6 5.3 fusion.806
  540.4 5.6 collective-permute-start.10
  546.5 5.4 collective-permute-start.8
  559.5 91.0 %reduce-scatter.2.cloned.1.call-done = f32[3,16]{0,1:T(8,128)} async-done(((f32[3,512]{0,1:T(8,128)}), f32[3,16]{0,1:T(8,128)}) %reduce-scatter.2.cloned.1.call-update) | async-done | bytes 208 | tf_op jit(solution)/shard_map/reduce_scatter | solution.py:218
  663.3 5.9 copy.2200
  674.1 5.0 copy.2201
  679.1 5.0 copy.2202
  684.1 23.7 %pad_maximum_fusion.1 = f32[15,9,3072]{1,0,2:T(8,128)} fusion(f32[15,9,768]{1,0,2:T(8,128)} %copy.2202, f32[15,9,768]{1,0,2:T(8,128)} %copy.2201, f32[15,9,768]{1,0,2:T(8,128)} %copy.2200, f32[15,9,768]{1,0,2:T(8,128)} %copy.2199), kind=kLoop, calls=%fused_computation.20 | loop fusion | flops 1244160 | bytes 3317760 | tf_op jit(solution)/shard_map/concatenate | solution.py:91
  707.8 11.1 %gather_fusion.16 = f32[512,15,9]{2,1,0:T(8,128)} fusion(f32[15,9,3072]{1,0,2:T(8,128)} %pad_maximum_fusion.1, s32[1024]{0:T(1024)S(1)} %copy-done.298), kind=kCustom, calls=%fused_computation.15.clone | custom fusion | bytes 555008 | tf_op jit(solution)/shard_map/jit(_take)/gather | solution.py:103
  726.2 11.1 %gather_fusion.15 = f32[512,15,9]{2,1,0:T(8,128)} fusion(f32[15,9,3072]{1,0,2:T(8,128)} %pad_maximum_fusion.1, s32[1024]{0:T(1024)S(1)} %copy-done.296), kind=kCustom, calls=%fused_computation.14.clone | custom fusion | bytes 555008 | tf_op jit(solution)/shard_map/jit(_take)/gather | solution.py:103
  744.5 11.1 %gather_fusion.14 = f32[512,15,9]{2,1,0:T(8,128)} fusion(f32[15,9,3072]{1,0,2:T(8,128)} %pad_maximum_fusion.1, s32[1024]{0:T(1024)S(1)} %copy-done.294), kind=kCustom, calls=%fused_computation.13.clone | custom fusion | bytes 555008 | tf_op jit(solution)/shard_map/jit(_take)/gather | solution.py:103
  755.6 11.1 %gather_fusion.13 = f32[512,15,9]{2,1,0:T(8,128)} fusion(f32[15,9,3072]{1,0,2:T(8,128)} %pad_maximum_fusion.1, s32[1024]{0:T(1024)S(1)} %copy-done.292), kind=kCustom, calls=%fused_computation.12.clone | custom fusion | bytes 555008 | tf_op jit(solution)/shard_map/jit(_take)/gather | solution.py:103
  806.1 5.1 copy_subtract_fusion
  (1209 shorter events, 490.5 us)
Async XLA Ops:
  7.2 643.3 %reduce-scatter.2.cloned.1.call-start = ((), (), s32[]{:S(2)}) async-start(), calls=%async_computation.1 | async-start | bytes 270336 | tf_op jit(solution)/shard_map/reduce_scatter | solution.py:218
  8.6 177.4 %collective-permute-start.4 = (s32[64]{0:T(128)}, s32[64]{0:T(128)}, u32[]{:S(2)}, u32[]{:S(2)}) collective-permute-start(s32[64]{0:T(128)} %get-tuple-element.514), channel_id=1, source_target_pairs={{0,8},{8,16},{16,24},{1,9},{9,17},{17,25},{2,10},{10,18},{18,26},{... | collective-permute-start | bytes 776 | tf_op jit(solution)/shard_map/ppermute | solution.py:17
  11.5 179.5 %collective-permute-start.5 = (s32[64]{0:T(128)}, s32[64]{0:T(128)}, u32[]{:S(2)}, u32[]{:S(2)}) collective-permute-start(s32[64]{0:T(128)} %get-tuple-element.515), channel_id=1, source_target_pairs={{8,0},{16,8},{24,16},{9,1},{17,9},{25,17},{10,2},{18,10},{26,18},{... | collective-permute-start | bytes 776 | tf_op jit(solution)/shard_map/ppermute | solution.py:17
  12.8 181.1 %collective-permute-start.7 = (s32[64]{0:T(128)}, s32[64]{0:T(128)}, u32[]{:S(2)}, u32[]{:S(2)}) collective-permute-start(s32[64]{0:T(128)} %get-tuple-element.516), channel_id=1, source_target_pairs={{1,0},{2,1},{3,2},{4,3},{5,4},{6,5},{7,6},{9,8},{10,9},{11,10},{12... | collective-permute-start | bytes 776 | tf_op jit(solution)/shard_map/ppermute | solution.py:17
  14.1 181.5 %collective-permute-start.6 = (s32[64]{0:T(128)}, s32[64]{0:T(128)}, u32[]{:S(2)}, u32[]{:S(2)}) collective-permute-start(s32[64]{0:T(128)} %get-tuple-element.517), channel_id=1, source_target_pairs={{0,1},{1,2},{2,3},{3,4},{4,5},{5,6},{6,7},{8,9},{9,10},{10,11},{11... | collective-permute-start | bytes 776 | tf_op jit(solution)/shard_map/ppermute | solution.py:17
  85.0 47.7 %copy-start.335 = (pred[64]{0:T(512)(128)(4,1)}, pred[64]{0:T(512)(128)(4,1)S(1)}, u32[]{:S(2)}) copy-start(pred[64]{0:T(512)(128)(4,1)S(1)} %get-tuple-element.28) | copy-start | bytes 196
  85.0 42.9 %copy-start.326 = (s32[1024]{0:T(1024)}, s32[1024]{0:T(1024)S(1)}, u32[]{:S(2)}) copy-start(s32[1024]{0:T(1024)S(1)} %pad_clamp_fusion.4) | copy-start | bytes 12292
  86.0 57.3 %copy-start.2 = (bf16[1,35,9,512]{3,0,2,1:T(2,128)(2,1)}, bf16[1,35,9,512]{3,0,2,1:T(2,128)(2,1)S(1)}, u32[]{:S(2)}) copy-start(bf16[1,35,9,512]{3,0,2,1:T(2,128)(2,1)S(1)} %get-tuple-element.280) | copy-start | bytes 967684
  133.4 77.4 %collective-permute-start.3 = (f32[35,9,64]{2,0,1:T(8,128)}, f32[35,9,64]{2,0,1:T(8,128)}, u32[]{:S(2)}, u32[]{:S(2)}) collective-permute-start(f32[35,9,64]{2,0,1:T(8,128)} %select_bitcast_fusion.4), channel_id=1, source_target_pairs={{1,0},{2,1},{3,2},{4,3},{5,4},{6,5},{7,6},{9,8},{10,9},{11,10},{12... | collective-permute-start | bytes 241928 | tf_op jit(solution)/shard_map/ppermute | solution.py:17
  140.7 30.3 %copy-start.327 = (s32[1024]{0:T(1024)}, s32[1024]{0:T(1024)S(1)}, u32[]{:S(2)}) copy-start(s32[1024]{0:T(1024)S(1)} %pad_clamp_fusion.6) | copy-start | bytes 12292
  141.4 26.6 %copy-start.328 = (s32[1024]{0:T(1024)}, s32[1024]{0:T(1024)S(1)}, u32[]{:S(2)}) copy-start(s32[1024]{0:T(1024)S(1)} %pad_clamp_fusion.5) | copy-start | bytes 12292
  186.1 24.8 %collective-permute-start.2 = (f32[35,9,64]{2,0,1:T(8,128)S(1)}, f32[35,9,64]{2,0,1:T(8,128)S(1)}, u32[]{:S(2)}, u32[]{:S(2)}) collective-permute-start(f32[35,9,64]{2,0,1:T(8,128)S(1)} %select_bitcast_fusion.5), channel_id=1, source_target_pairs={{0,1},{1,2},{2,3},{3,4},{4,5},{5,6},{6,7},{8,9},{9,10},{10,11},{11... | collective-permute-start | bytes 241928 | tf_op jit(solution)/shard_map/ppermute | solution.py:17
  191.0 19.8 %collective-permute-start = (f32[35,9,64]{2,0,1:T(8,128)S(1)}, f32[35,9,64]{2,0,1:T(8,128)S(1)}, u32[]{:S(2)}, u32[]{:S(2)}) collective-permute-start(f32[35,9,64]{2,0,1:T(8,128)S(1)} %select_bitcast_fusion.7), channel_id=1, source_target_pairs={{0,8},{8,16},{16,24},{1,9},{9,17},{17,25},{2,10},{10,18},{18,26},{... | collective-permute-start | bytes 241928 | tf_op jit(solution)/shard_map/ppermute | solution.py:17
  194.0 18.2 %collective-permute-start.1 = (f32[35,9,64]{2,0,1:T(8,128)S(1)}, f32[35,9,64]{2,0,1:T(8,128)}, u32[]{:S(2)}, u32[]{:S(2)}) collective-permute-start(f32[35,9,64]{2,0,1:T(8,128)S(1)} %select_bitcast_fusion.6), channel_id=1, source_target_pairs={{8,0},{16,8},{24,16},{9,1},{17,9},{25,17},{10,2},{18,10},{26,18},{... | collective-permute-start | bytes 241928 | tf_op jit(solution)/shard_map/ppermute | solution.py:17
  209.6 75.0 %copy-start.301 = (pred[512]{0:T(512)(128)(4,1)}, pred[512]{0:T(512)(128)(4,1)S(1)}, u32[]{:S(2)}) copy-start(pred[512]{0:T(512)(128)(4,1)S(1)} %compare_and_fusion) | copy-start | bytes 1540
  210.7 92.0 %copy-start.309 = (pred[512]{0:T(512)(128)(4,1)}, pred[512]{0:T(512)(128)(4,1)S(1)}, u32[]{:S(2)}) copy-start(pred[512]{0:T(512)(128)(4,1)S(1)} %get-tuple-element.583) | copy-start | bytes 1540
  210.8 58.5 %copy-start.297 = (s32[1024]{0:T(1024)}, s32[1024]{0:T(1024)S(1)}, u32[]{:S(2)}) copy-start(s32[1024]{0:T(1024)S(1)} %get-tuple-element.579) | copy-start | bytes 12292
  210.8 76.8 %copy-start.295 = (s32[1024]{0:T(1024)}, s32[1024]{0:T(1024)S(1)}, u32[]{:S(2)}) copy-start(s32[1024]{0:T(1024)S(1)} %get-tuple-element.580) | copy-start | bytes 12292
  210.8 94.9 %copy-start.293 = (s32[1024]{0:T(1024)}, s32[1024]{0:T(1024)S(1)}, u32[]{:S(2)}) copy-start(s32[1024]{0:T(1024)S(1)} %get-tuple-element.581) | copy-start | bytes 12292
  210.8 106.0 %copy-start.291 = (s32[1024]{0:T(1024)}, s32[1024]{0:T(1024)S(1)}, u32[]{:S(2)}) copy-start(s32[1024]{0:T(1024)S(1)} %get-tuple-element.582) | copy-start | bytes 12292
  537.0 114.8 %collective-permute-start.11 = (f32[35,9,64]{2,0,1:T(8,128)}, f32[35,9,64]{2,0,1:T(8,128)}, u32[]{:S(2)}, u32[]{:S(2)}) collective-permute-start(f32[35,9,64]{2,0,1:T(8,128)} %select_bitcast_fusion), channel_id=1, source_target_pairs={{1,0},{2,1},{3,2},{4,3},{5,4},{6,5},{7,6},{9,8},{10,9},{11,10},{12... | collective-permute-start | bytes 241928 | tf_op jit(solution)/shard_map/ppermute | solution.py:17
  540.4 111.4 %collective-permute-start.10 = (f32[35,9,64]{2,0,1:T(8,128)}, f32[35,9,64]{2,0,1:T(8,128)}, u32[]{:S(2)}, u32[]{:S(2)}) collective-permute-start(f32[35,9,64]{2,0,1:T(8,128)} %select_bitcast_fusion.1), channel_id=1, source_target_pairs={{0,1},{1,2},{2,3},{3,4},{4,5},{5,6},{6,7},{8,9},{9,10},{10,11},{11... | collective-permute-start | bytes 241928 | tf_op jit(solution)/shard_map/ppermute | solution.py:17
  546.5 105.2 %collective-permute-start.8 = (f32[35,9,64]{2,0,1:T(8,128)S(1)}, f32[35,9,64]{2,0,1:T(8,128)S(1)}, u32[]{:S(2)}, u32[]{:S(2)}) collective-permute-start(f32[35,9,64]{2,0,1:T(8,128)S(1)} %select_bitcast_fusion.3), channel_id=1, source_target_pairs={{0,8},{8,16},{16,24},{1,9},{9,17},{17,25},{2,10},{10,18},{18,26},{... | collective-permute-start | bytes 241928 | tf_op jit(solution)/shard_map/ppermute | solution.py:17
  552.0 100.5 %collective-permute-start.9 = (f32[35,9,64]{2,0,1:T(8,128)S(1)}, f32[35,9,64]{2,0,1:T(8,128)}, u32[]{:S(2)}, u32[]{:S(2)}) collective-permute-start(f32[35,9,64]{2,0,1:T(8,128)S(1)} %select_bitcast_fusion.2), channel_id=1, source_target_pairs={{8,0},{16,8},{24,16},{9,1},{17,9},{25,17},{10,2},{18,10},{26,18},{... | collective-permute-start | bytes 241928 | tf_op jit(solution)/shard_map/ppermute | solution.py:17
  (328 other events, 1217.5 us)
Sparse Core Ops, SparseCore 0:
  511.6 138.8 reduce-scatter.1
where the time goes:
time: 831 us; the launch traced here: 818 us
  local copies, waits for them, and re-layouts  434 us (52%)
  other arithmetic  192 us (23%)
  waiting for transfers between devices  91 us (11%)
  matrix products  46.3 us (6%)
  starting transfers between devices  35.7 us (4%)
  between operations  19.8 us (2%)
    gather x16, local copies, waits for them, and re-layouts, apply_faces(): jnp.take(traces, flat_index[face], axis=2)  123 us
    slice x27, local copies, waits for them, and re-layouts, star_apply(): field[:, 2]  103 us
    reduce_scatter x1, waiting for transfers between devices, shards(): lax.psum_scatter(step_hist, ('depth', 'map'), scatter_dimension=1, tiled=...  91 us
    unnamed x179, other arithmetic  52.2 us
    reshape x16, local copies, waits for them, and re-layouts, one_face(): jnp.dot(face_basis[face].T, flat, precision=HIGH)  49.4 us
    concatenate x2, other arithmetic, all_face_traces(): jnp.concatenate([one_face(flat, face_basis, face, fields, width) for face...  47.4 us
    unnamed x721, local copies, waits for them, and re-layouts  37.8 us
    ppermute x12, starting transfers between devices, shifted(): lax.ppermute(value, axis, [(source, source + steps) for source in range(i...  35.7 us
  transfers between devices with their start and end apart: 13, of which 1 were waited for; matrix products, arithmetic and copies ran while one was open for 24% of the time, Pallas kernels for 0%

commit v1 on v0

v1 whole, which is shorter than its diff:
```python
import functools

import jax
import jax.numpy as jnp
from jax import lax
from jax.experimental import pallas as pl
from jax.experimental.pallas import tpu as pltpu
from jax.sharding import PartitionSpec as P

MESH = pl.DeviceIdType.MESH
PICARD = 4
HALF = 0.15
FULL = 0.3
KERNEL_WEIGHT = 0.125
F32 = jnp.float32
BF16 = jnp.bfloat16
ROWS = 40
KROWS = 48
TRACE = 144


def split(value):
    high = value.astype(BF16)
    low = (value - high.astype(F32)).astype(BF16)
    return high, low


def wide_dot(left, right):
    return jnp.dot(left, right, preferred_element_type=F32)


def kernel(
    n_depth,
    n_map,
    adj_ref,
    fwd_ref,
    p_ref,
    s_ref,
    rho_ref,
    jac_ref,
    ang_ref,
    scale_ref,
    amat_ref,
    lmat_ref,
    nbr_ref,
    nface_ref,
    send_ref,
    cell_ref,
    out_ref,
    hist_ref,
    q_buf,
    p_buf,
    b_buf,
    y_buf,
    f_buf,
    coef,
    onehot,
    send_hot,
    left_buf,
    ghost_left,
    far_buf,
    flux_buf,
    fx_buf,
    sums,
    send_buf,
    recv_buf,
    cells_out,
    cells_main,
    cells_side,
    g_send,
    g_recv,
    h_send,
    h_recv_main,
    h_recv_side,
):
    n_dev = n_depth * n_map
    count = adj_ref.shape[2]
    basis = adj_ref.shape[1]
    steps = fwd_ref.shape[0]
    tiles = count // 128
    per_dev = count // 32
    total_cells = per_dev * n_dev
    own_i = lax.axis_index("depth")
    own_j = lax.axis_index("map")
    me = own_i * n_map + own_j

    def place(linear):
        return (lax.div(linear, n_map), lax.rem(linear, n_map))

    links = [
        (0, 0, own_i < n_depth - 1, (own_i + 1, own_j), own_i > 0, (own_i - 1, own_j)),
        (1, 0, own_i > 0, (own_i - 1, own_j), own_i < n_depth - 1, (own_i + 1, own_j)),
        (2, 1, own_j < n_map - 1, (own_i, own_j + 1), own_j > 0, (own_i, own_j - 1)),
        (3, 1, own_j > 0, (own_i, own_j - 1), own_j < n_map - 1, (own_i, own_j + 1)),
    ]

    recv_buf[...] = jnp.zeros_like(recv_buf)
    cells_main[...] = jnp.zeros_like(cells_main)
    cells_side[...] = jnp.zeros_like(cells_side)

    barrier = pltpu.get_barrier_semaphore()
    for slot, tile, to_ok, target, from_ok, source in links:

        @pl.when(from_ok)
        def _(source=source):
            pl.semaphore_signal(barrier, inc=1, device_id=source, device_id_type=MESH)

    def main_source(j):
        return lax.div(me + n_dev * j, per_dev)

    def side_source(j):
        cell = me + n_dev * j
        place_in = lax.rem(cell, per_dev)
        home = lax.div(cell, per_dev)
        below = jnp.logical_and(place_in == 0, home > 0)
        above = jnp.logical_and(place_in == per_dev - 1, home < n_dev - 1)
        source = jnp.where(below, home - 1, home + 1)
        return jnp.logical_or(below, above), jnp.clip(source, 0, n_dev - 1)

    def greet(j, carry):
        main = main_source(j)

        @pl.when(main != me)
        def _():
            pl.semaphore_signal(barrier, inc=1, device_id=place(main), device_id_type=MESH)

        exists, side = side_source(j)

        @pl.when(jnp.logical_and(exists, side != me))
        def _():
            pl.semaphore_signal(barrier, inc=1, device_id=place(side), device_id_type=MESH)

        return carry

    lax.fori_loop(0, per_dev, greet, 0)

    p_speed, s_speed, density = p_ref[...], s_ref[...], rho_ref[...]
    lame = density * (p_speed * p_speed - 2.0 * s_speed * s_speed)
    shear = density * s_speed * s_speed
    inv_rho = 1.0 / density

    def keep(index, row):
        coef[index] = jnp.broadcast_to(row, (8, count))

    for d in range(3):
        for a in range(3):
            row = jac_ref[d, a : a + 1, :]
            keep(d * 3 + a, row)
            keep(9 + d * 3 + a, HALF * inv_rho * row)
    keep(18, HALF * lame)
    keep(19, 2.0 * HALF * shear)
    keep(20, HALF * shear)
    azimuth, polar = ang_ref[0], ang_ref[1]
    sin_polar = jnp.sin(polar)
    normal = [jnp.cos(azimuth) * sin_polar, jnp.sin(azimuth) * sin_polar, jnp.cos(polar)]
    weight = (0.5 * FULL) * scale_ref[...]
    for f in range(4):
        for a in range(3):
            keep(21 + f * 3 + a, weight[f : f + 1] * normal[a][f : f + 1])
        keep(37 + f, weight[f : f + 1] * p_speed)
    keep(33, lame)
    keep(34, 2.0 * shear)
    keep(35, shear)
    keep(36, inv_rho)

    ghosts = 256
    locals_all = 4 * count
    row_ids = lax.broadcasted_iota(jnp.int32, (256, count), 0)
    for f in range(4):
        nbr = nbr_ref[f : f + 1, :]
        local = nface_ref[f : f + 1, :] * count + nbr
        outer = jnp.where(nbr < count + ghosts, nbr - count + locals_all, -1)
        index = jnp.where(nbr < count, local, outer)
        for block in range((locals_all + ghosts) // 256):
            hit = (row_ids + block * 256) == index
            onehot[block * 256 : (block + 1) * 256, f * count : (f + 1) * count] = jnp.where(
                hit, 1.0, 0.0
            ).astype(BF16)
    send_ids = lax.broadcasted_iota(jnp.int32, (256, ghosts), 0)
    for block in range(locals_all // 256):
        hit = (send_ids + block * 256) == send_ref[...]
        send_hot[block * 256 : (block + 1) * 256, :] = jnp.where(hit, 1.0, 0.0).astype(BF16)

    q_buf[:, 32:ROWS, :] = jnp.zeros((9, 8, count), F32)
    f_buf[:, 32:ROWS, :] = jnp.zeros((9, 8, count), F32)
    q_buf[:, 0:basis, :] = adj_ref[...]
    b_buf[...] = jnp.zeros_like(b_buf)
    sums[...] = jnp.zeros_like(sums)

    def load_operand(source):
        for field in range(9):
            high, low = split(source[field])
            b_buf[field, 0:ROWS, :] = high
            b_buf[field, KROWS : KROWS + ROWS, :] = low
            b_buf[field, 2 * KROWS : 2 * KROWS + ROWS, :] = high

    def volume(rows):
        for field in range(9):
            y_buf[field, 0:rows, :] = wide_dot(amat_ref[0:rows, :], b_buf[field])

    def advance(factor):
        for t in range(tiles):
            lanes = slice(t * 128, (t + 1) * 128)
            lame_c = coef[18, :, lanes] * factor
            two_c = coef[19, :, lanes] * factor
            shear_c = coef[20, :, lanes] * factor
            for r in range(ROWS // 8):
                rows = slice(r * 8, r * 8 + 8)

                def moved(d, field):
                    return y_buf[field, d * ROWS + r * 8 : d * ROWS + r * 8 + 8, lanes]

                grad = {}
                for b in range(3):
                    parts = [moved(d, 6 + b) for d in range(3)]
                    for a in range(3):
                        grad[a, b] = (
                            coef[a, :, lanes] * parts[0]
                            + coef[3 + a, :, lanes] * parts[1]
                            + coef[6 + a, :, lanes] * parts[2]
                        )
                dil = lame_c * (grad[0, 0] + grad[1, 1] + grad[2, 2])
                for a in range(3):
                    p_buf[a, rows, lanes] = q_buf[a, rows, lanes] - dil - two_c * grad[a, a]
                for field, a, b in ((3, 0, 1), (4, 1, 2), (5, 0, 2)):
                    p_buf[field, rows, lanes] = q_buf[field, rows, lanes] - shear_c * (
                        grad[a, b] + grad[b, a]
                    )
                stress = [[moved(d, field) for d in range(3)] for field in range(6)]
                for b, picks in ((0, (0, 3, 5)), (1, (3, 1, 4)), (2, (5, 4, 2))):
                    total = None
                    for d in range(3):
                        for a in range(3):
                            term = coef[9 + d * 3 + a, :, lanes] * stress[picks[a]][d]
                            total = term if total is None else total + term
                    p_buf[6 + b, rows, lanes] = q_buf[6 + b, rows, lanes] - factor * total

    def element_sums(step):
        for field in range(9):
            f_buf[field, 0:basis, :] = fwd_ref[step, field].astype(F32)
        for t in range(tiles):
            lanes = slice(t * 128, (t + 1) * 128)
            first, second, third = None, None, None
            for r in range(ROWS // 8):
                rows = slice(r * 8, r * 8 + 8)
                x = [p_buf[field, rows, lanes] for field in range(9)]
                y = [f_buf[field, rows, lanes] for field in range(9)]
                one = (x[0] + x[1] + x[2]) * (y[0] + y[1] + y[2])
                two = (x[0] * y[0] + x[1] * y[1] + x[2] * y[2]) + 2.0 * (
                    x[3] * y[3] + x[4] * y[4] + x[5] * y[5]
                )
                three = x[6] * y[6] + x[7] * y[7] + x[8] * y[8]
                first = one if first is None else first + one
                second = two if second is None else second + two
                third = three if third is None else third + three
            sums[0, :, lanes] += first
            sums[1, :, lanes] += second
            sums[2, :, lanes] += third

    def ghost_copy(step, link):
        slot, tile, to_ok, target, from_ok, source = link
        return pltpu.make_async_remote_copy(
            src_ref=send_buf.at[step, tile],
            dst_ref=recv_buf.at[step, slot],
            send_sem=g_send.at[step, slot],
            recv_sem=g_recv.at[step, slot],
            device_id=target,
            device_id_type=MESH,
        )

    pl.semaphore_wait(
        barrier,
        sum(link[2].astype(jnp.int32) for link in links) + target_count(me, n_dev, per_dev),
    )

    def step_body(step, carry):
        load_operand(q_buf)

        def sweep(_, inner):
            volume(3 * ROWS)
            advance(1.0)
            load_operand(p_buf)
            return inner

        lax.fori_loop(0, PICARD, sweep, 0)
        element_sums(step)
        volume(3 * ROWS + 64)
        base = 3 * ROWS
        for field in range(9):
            for g in range(4):
                high, low = split(y_buf[field, base + g * 16 : base + g * 16 + 16, :])
                columns = slice(g * count, (g + 1) * count)
                left_buf[field * 16 : field * 16 + 16, columns] = high
                left_buf[TRACE + field * 16 : TRACE + field * 16 + 16, columns] = low
        picked = wide_dot(left_buf[...], send_hot[...])
        picked = picked[0:TRACE] + picked[TRACE:]
        for tile in range(2):
            send_buf[step, tile] = picked[:, tile * 128 : (tile + 1) * 128]
        for link in links:

            @pl.when(link[2])
            def _(link=link):
                ghost_copy(step, link).start()

        advance(2.0)
        for f in range(4):
            columns = slice(f * count, (f + 1) * count)
            got = wide_dot(left_buf[...], onehot[0:locals_all, columns])
            far_buf[:, columns] = got[0:TRACE] + got[TRACE:]

        for link in links:

            @pl.when(link[4])
            def _(link=link):
                ghost_copy(step, link).wait_recv()

        lane = lax.broadcasted_iota(jnp.int32, (TRACE, 128), 1)
        for tile in range(2):
            both = jnp.where(lane < 64, recv_buf[step, 2 * tile], recv_buf[step, 2 * tile + 1])
            high, low = split(both)
            ghost_left[0:TRACE, tile * 128 : (tile + 1) * 128] = high
            ghost_left[TRACE:, tile * 128 : (tile + 1) * 128] = low
        for f in range(4):
            columns = slice(f * count, (f + 1) * count)
            got = wide_dot(ghost_left[...], onehot[locals_all:, columns])
            far_buf[:, columns] += got[0:TRACE] + got[TRACE:]

        for f in range(4):
            for t in range(tiles):
                lanes = slice(t * 128, (t + 1) * 128)
                far_lanes = slice(f * count + t * 128, f * count + (t + 1) * 128)
                nx, ny, nz = (coef[21 + f * 3 + a, :, lanes] for a in range(3))
                lame_c, two_c = coef[33, :, lanes], coef[34, :, lanes]
                shear_c, inv_c = coef[35, :, lanes], coef[36, :, lanes]
                speed = coef[37 + f, :, lanes]
                for r in range(2):
                    own = [
                        y_buf[k, base + f * 16 + r * 8 : base + f * 16 + r * 8 + 8, lanes]
                        for k in range(9)
                    ]
                    far = [
                        far_buf[k * 16 + r * 8 : k * 16 + r * 8 + 8, far_lanes] for k in range(9)
                    ]
                    x = [own[k] + far[k] for k in range(9)]
                    jump = [speed * (own[k] - far[k]) for k in range(9)]
                    gx, gy, gz = nx * x[6], ny * x[7], nz * x[8]
                    dil = lame_c * (gx + gy + gz)
                    flux = [
                        jump[0] - dil - two_c * gx,
                        jump[1] - dil - two_c * gy,
                        jump[2] - dil - two_c * gz,
                        jump[3] - shear_c * (ny * x[6] + nx * x[7]),
                        jump[4] - shear_c * (nz * x[7] + ny * x[8]),
                        jump[5] - shear_c * (nz * x[6] + nx * x[8]),
                        jump[6] - inv_c * (nx * x[0] + ny * x[3] + nz * x[5]),
                        jump[7] - inv_c * (nx * x[3] + ny * x[1] + nz * x[4]),
                        jump[8] - inv_c * (nx * x[5] + ny * x[4] + nz * x[2]),
                    ]
                    for k in range(9):
                        flux_buf[k, f * 16 + r * 8 : f * 16 + r * 8 + 8, lanes] = flux[k]
        for field in range(9):
            high, low = split(flux_buf[field])
            fx_buf[0:64, :] = high
            fx_buf[64:128, :] = low
            fx_buf[128:192, :] = high
            q_buf[field] = p_buf[field] - wide_dot(lmat_ref[...], fx_buf[...])
        for link in links:

            @pl.when(link[2])
            def _(link=link):
                ghost_copy(step, link).wait_send()

        return carry

    lax.fori_loop(0, steps, step_body, 0)
    out_ref[...] = q_buf[:, 0:basis, :]

    parts = [jnp.sum(sums[k], axis=0, keepdims=True) for k in range(3)]
    first, second, third = parts
    gain = KERNEL_WEIGHT * FULL
    square = s_speed * s_speed
    terms = [
        gain * (2.0 * density * p_speed * first),
        gain * (density * s_speed * (2.0 * second - 4.0 * first)),
        gain * ((p_speed * p_speed - 2.0 * square) * first + square * second + third),
    ]
    term_row = lax.broadcasted_iota(jnp.int32, (8, count), 0)
    stacked = jnp.where(term_row == 0, terms[0], 0.0)
    stacked = jnp.where(term_row == 1, terms[1], stacked)
    stacked = jnp.where(term_row == 2, terms[2], stacked)
    entry = cell_ref[...]
    owner = lax.shift_right_logical(entry, per_dev.bit_length() - 1)
    coarse = (entry - owner * per_dev) * n_dev + owner
    relative = coarse - (per_dev * me - 1)
    hot = jnp.where(
        lax.broadcasted_iota(jnp.int32, (128, count), 0) == relative, 1.0, 0.0
    ).astype(F32)
    cells_out[...] = lax.dot_general(
        stacked,
        hot,
        (((1,), (1,)), ((), ())),
        precision=lax.Precision.HIGHEST,
        preferred_element_type=F32,
    )

    def cell_copy(c, cell, dst, sem):
        target = lax.rem(cell, n_dev)
        slot = lax.div(cell, n_dev)
        return pltpu.make_async_remote_copy(
            src_ref=cells_out,
            dst_ref=dst.at[slot],
            send_sem=h_send.at[c],
            recv_sem=sem.at[slot],
            device_id=place(target),
            device_id_type=MESH,
        )

    def to_cell(c, cell, dst, sem):
        target = lax.rem(cell, n_dev)
        slot = lax.div(cell, n_dev)

        @pl.when(target != me)
        def _():
            cell_copy(c, cell, dst, sem).start()

        @pl.when(target == me)
        def _():
            dst[slot] = cells_out[...]

    low_cell = per_dev * me - 1
    high_cell = per_dev * me + per_dev

    def send_main(c, carry):
        to_cell(c, per_dev * me + c, cells_main, h_recv_main)
        return carry

    lax.fori_loop(0, per_dev, send_main, 0)

    @pl.when(me > 0)
    def _():
        to_cell(per_dev, low_cell, cells_side, h_recv_side)

    @pl.when(me < n_dev - 1)
    def _():
        to_cell(per_dev + 1, high_cell, cells_side, h_recv_side)

    def finish(j, carry):
        @pl.when(main_source(j) != me)
        def _():
            pltpu.make_async_copy(cells_out, cells_main.at[j], h_recv_main.at[j]).wait()

        exists, side = side_source(j)

        @pl.when(jnp.logical_and(exists, side != me))
        def _():
            pltpu.make_async_copy(cells_out, cells_side.at[j], h_recv_side.at[j]).wait()

        return carry

    lax.fori_loop(0, per_dev, finish, 0)

    lane = lax.broadcasted_iota(jnp.int32, (8, 128), 1)
    inner = lax.rem(me, per_dev)
    main_lane = inner + 1
    side_lane = jnp.where(inner == 0, per_dev + 1, 0)
    result = jnp.zeros((8, 128), F32)
    for j in range(per_dev):
        value = jnp.where(lane == main_lane, cells_main[j], 0.0)
        value = value + jnp.where(lane == side_lane, cells_side[j], 0.0)
        result = jnp.where(lane == j, jnp.sum(value, axis=1, keepdims=True), result)
    hist_ref[...] = result[0:3, 0:per_dev]

    def drain(c, carry):
        @pl.when(lax.rem(per_dev * me + c, n_dev) != me)
        def _():
            pltpu.make_async_copy(cells_out, cells_main.at[0], h_send.at[c]).wait()

        return carry

    lax.fori_loop(0, per_dev, drain, 0)

    @pl.when(jnp.logical_and(me > 0, lax.rem(jnp.maximum(low_cell, 0), n_dev) != me))
    def _():
        pltpu.make_async_copy(cells_out, cells_side.at[0], h_send.at[per_dev]).wait()

    @pl.when(jnp.logical_and(me < n_dev - 1, lax.rem(high_cell, n_dev) != me))
    def _():
        pltpu.make_async_copy(cells_out, cells_side.at[0], h_send.at[per_dev + 1]).wait()


def target_count(me, n_dev, per_dev):
    total = jnp.int32(0)
    for c in range(per_dev):
        total = total + (lax.rem(per_dev * me + c, n_dev) != me).astype(jnp.int32)
    low_cell = per_dev * me - 1
    high_cell = per_dev * me + per_dev
    low = jnp.logical_and(me > 0, lax.rem(jnp.maximum(low_cell, 0), n_dev) != me)
    high = jnp.logical_and(me < n_dev - 1, lax.rem(high_cell, n_dev) != me)
    return total + low.astype(jnp.int32) + high.astype(jnp.int32)


def three_way(matrix):
    high = lax.reduce_precision(matrix, 8, 7)
    low = matrix - high
    return jnp.concatenate([high, high, low], axis=1).astype(BF16)


def shards(
    n_depth,
    n_map,
    adjoint,
    forward,
    p_speed,
    s_speed,
    density,
    inv_jacobian,
    face_angles,
    face_scale,
    stiffness,
    face_basis,
    neighbours,
    neighbour_face,
    send_elements,
    send_faces,
    cell_index,
):
    basis, fields, count = adjoint.shape
    steps = forward.shape[0]
    modes = face_basis.shape[2]
    per_dev = count // 32
    moving = jnp.pad(
        jnp.transpose(stiffness, (0, 2, 1)), ((0, 0), (0, ROWS - basis), (0, KROWS - basis))
    ).reshape(3 * ROWS, KROWS)
    tracing = jnp.pad(
        jnp.transpose(face_basis, (0, 2, 1)), ((0, 0), (0, 16 - modes), (0, KROWS - basis))
    ).reshape(64, KROWS)
    amat = three_way(jnp.concatenate([moving, tracing], axis=0))
    lifting = jnp.pad(
        jnp.transpose(face_basis, (1, 0, 2)), ((0, ROWS - basis), (0, 0), (0, 16 - modes))
    ).reshape(ROWS, 64)
    lmat = three_way(lifting)
    send_index = (send_faces * count + send_elements).reshape(1, 256)
    row = lambda value: value.reshape(1, count)
    vmem = pl.BlockSpec(memory_space=pltpu.VMEM)
    state, kernels = pl.pallas_call(
        functools.partial(kernel, n_depth, n_map),
        out_shape=(
            jax.ShapeDtypeStruct((fields, basis, count), F32),
            jax.ShapeDtypeStruct((3, per_dev), F32),
        ),
        in_specs=[vmem] * 14,
        out_specs=(vmem, vmem),
        scratch_shapes=[
            pltpu.VMEM((9, ROWS, count), F32),
            pltpu.VMEM((9, ROWS, count), F32),
            pltpu.VMEM((9, 3 * KROWS, count), BF16),
            pltpu.VMEM((9, 3 * ROWS + 64, count), F32),
            pltpu.VMEM((9, ROWS, count), F32),
            pltpu.VMEM((41, 8, count), F32),
            pltpu.VMEM((4 * count + 256, 4 * count), BF16),
            pltpu.VMEM((4 * count, 256), BF16),
            pltpu.VMEM((2 * TRACE, 4 * count), BF16),
            pltpu.VMEM((2 * TRACE, 256), BF16),
            pltpu.VMEM((TRACE, 4 * count), F32),
            pltpu.VMEM((9, 64, count), F32),
            pltpu.VMEM((192, count), BF16),
            pltpu.VMEM((3, 8, count), F32),
            pltpu.VMEM((steps, 2, TRACE, 128), F32),
            pltpu.VMEM((steps, 4, TRACE, 128), F32),
            pltpu.VMEM((8, 128), F32),
            pltpu.VMEM((per_dev, 8, 128), F32),
            pltpu.VMEM((per_dev, 8, 128), F32),
            pltpu.SemaphoreType.DMA((steps, 4)),
            pltpu.SemaphoreType.DMA((steps, 4)),
            pltpu.SemaphoreType.DMA((per_dev + 2,)),
            pltpu.SemaphoreType.DMA((per_dev,)),
            pltpu.SemaphoreType.DMA((per_dev,)),
        ],
        compiler_params=pltpu.CompilerParams(
            collective_id=0, has_side_effects=True, vmem_limit_bytes=56 * 1024 * 1024
        ),
    )(
        jnp.transpose(adjoint, (1, 0, 2)),
        jnp.transpose(forward, (0, 2, 1, 3)),
        row(p_speed),
        row(s_speed),
        row(density),
        inv_jacobian,
        face_angles,
        face_scale,
        amat,
        lmat,
        neighbours,
        neighbour_face,
        send_index,
        row(cell_index),
    )
    return jnp.transpose(state, (1, 0, 2)), kernels


def solution(mesh):
    n_depth, n_map = mesh.shape["depth"], mesh.shape["map"]
    both = ("depth", "map")
    placed = (
        P(None, None, both),
        P(None, None, None, both),
        P(both),
        P(both),
        P(both),
        P(None, None, both),
        P(None, None, both),
        P(None, both),
        P(),
        P(),
        P(None, both),
        P(None, both),
        P(None, both),
        P(None, both),
        P(both),
    )
    return jax.shard_map(
        functools.partial(shards, n_depth, n_map),
        mesh=mesh,
        in_specs=placed,
        out_specs=(P(None, None, both), P(None, both)),
        check_vma=False,
    )
```

time: 831 us -> 45.8 us (0.06); the launches traced: 818 us -> 45.4 us
  local copies, waits for them, and re-layouts: 434 us -> 6.73 us
  other arithmetic: 192 us -> 2.24 us
  waiting for transfers between devices: 91 us -> 0 us
  matrix products: 46.3 us -> 0 us
  Pallas kernels: 0 us -> 35.8 us
  starting transfers between devices: 35.7 us -> 0 us
  between operations: 19.8 us -> 0.69 us
    gather x34 -> x0, local copies, waits for them, and re-layouts: 166 us -> none  [the longest x16 123 us: apply_faces(): jnp.take(traces, flat_index[face], axis=2)]
    slice x34 -> x0, local copies, waits for them, and re-layouts: 105 us -> none  [the longest x27 103 us: star_apply(): field[:, 2]]
    reduce_scatter x1 -> x0, waiting for transfers between devices: 91 us -> none  [shards(): lax.psum_scatter(step_hist, ('depth', 'map'), scatter_dimension=1, tiled=...]
    reshape x51 -> x2, local copies, waits for them, and re-layouts: 86 us -> 0.71 us  [the longest x1 0.64 us: shards(): send_index = (send_faces * count + send_elements).reshape(1, 256)]
    unnamed x179 -> x0, other arithmetic: 52.2 us -> none
    concatenate x3 -> x2, other arithmetic: 48.1 us -> 1.44 us  [three_way(): return jnp.concatenate([high, high, low], axis=1).astype(BF16)]
    dot_general x46 -> x0, matrix products: 46.3 us -> none  [the longest x30 30.2 us: volume_term(): jnp.dot(stiffness[coord].T, flat, precision=HIGH)]
    pallas_call x0 -> x1, Pallas kernels: none -> 35.8 us  [shards(): pl.pallas_call(functools.partial(kernel, n_depth, n_map), out_shape=(jax....]
  transfers between devices with their start and end apart: 13 -> 0, of which waited for: 1 -> 0; matrix products, arithmetic and copies ran while one was open for 24% -> 0% of each run, Pallas kernels for 0% -> 0%
where the time goes in v1:
time: 45.8 us; the launch traced here: 45.4 us
  Pallas kernels  35.8 us (78%)
  local copies, waits for them, and re-layouts  6.73 us (15%)
  other arithmetic  2.24 us (5%)
  between operations  0.69 us (2%)
    pallas_call x1, Pallas kernels, shards(): pl.pallas_call(functools.partial(kernel, n_depth, n_map), out_shape=(jax....  35.8 us
    unnamed x10, local copies, waits for them, and re-layouts  5.99 us
    concatenate x2, other arithmetic, three_way(): return jnp.concatenate([high, high, low], axis=1).astype(BF16)  1.44 us

profile of v1, /device:TPU:0, one launch (start us, length us, event | category | flops | bytes accessed | tf_op | source)
XLA Modules:
  0.0 45.4 jit_solution(17436560230868402336)
XLA Ops:
  0.6 0.0 copy-start
  0.6 0.8 %multiply_add_fusion = s32[4,64]{1,0:T(4,128)S(1)} fusion(s32[4,64]{1,0:T(4,128)} %param.27, s32[4,64]{1,0:T(4,128)} %param.28), kind=kLoop, calls=%fused_computation.10 | loop fusion | flops 512 | bytes 3072 | tf_op jit(solution)/shard_map/add | solution.py:542
  1.4 0.6 %reshape.34.send_ref = s32[1,256]{1,0:T(1,128)} reshape(s32[4,64]{1,0:T(4,128)S(1)} %multiply_add_fusion) | data formatting | bytes 2048 | tf_op jit(solution)/shard_map/reshape | solution.py:542
  2.1 0.8 %copy.28 = f32[4,15,35]{2,1,0:T(8,128)S(1)} copy(f32[4,15,35]{2,0,1:T(4,128)} %bitcast.21) | data formatting | bytes 16800
  2.8 0.8 %copy.29 = f32[35,4,15]{0,2,1:T(8,128)S(1)} copy(f32[35,4,15]{0,1,2:T(4,128)} %bitcast.22) | data formatting | bytes 16800
  3.6 0.1 copy.25
  3.7 0.7 %pad_maximum_fusion.2.lmat_ref = bf16[40,192]{1,0:T(8,128)(2,1)} fusion(bf16[40,64]{1,0:T(8,128)(2,1)S(1)} %get-tuple-element.9, bf16[40,64]{1,0:T(8,128)(2,1)S(1)} %get-tuple-element.8), kind=kLoop, calls=%fused_computation.9 | loop fusion | flops 46080 | bytes 25600 | tf_op jit(solution)/shard_map/concatenate | solution.py:505
  4.4 0.9 %copy.27 = f32[3,35,35]{2,1,0:T(8,128)S(1)} copy(f32[3,35,35]{1,2,0:T(8,128)} %bitcast.23) | data formatting | bytes 29400
  5.3 0.8 %pad_maximum_fusion.1.amat_ref = bf16[184,144]{1,0:T(8,128)(2,1)} fusion(bf16[184,48]{1,0:T(8,128)(2,1)S(1)} %get-tuple-element.7, bf16[184,48]{1,0:T(8,128)(2,1)S(1)} %get-tuple-element.6), kind=kLoop, calls=%fused_computation.5 | loop fusion | flops 158976 | bytes 88320 | tf_op jit(solution)/shard_map/concatenate | solution.py:505
  6.1 0.0 copy-done
  6.1 0.9 %copy.31 = bf16[2,35,9,512]{3,1,2,0:T(8,128)(2,1)} copy(bf16[2,35,9,512]{3,0,2,1:T(2,128)(2,1)S(1)} %copy-done) | data formatting | bytes 1290240 | tf_op args[1]
  7.0 35.8 %shard_map.158 = (f32[9,35,512]{2,1,0:T(8,128)}, f32[3,16]{1,0:T(4,128)}) custom-call(f32[9,35,512]{2,1,0:T(8,128)} %bitcast.16, bf16[2,9,35,512]{3,2,1,0:T(8,128)(2,1)} %bitcast.15, f32[1,512]{1,0:T(1,128)} %bitcast.24, f32[1,512]{1,0:T(1,128)} %bitcast.25, f32[1,512]{1,0:T(1,128)} %bitcast.26, f32[3,3,512]{2,1,0:T(4,128)} %jac_ref.1, ...), custom_call_target="tpu_custom_call" | custom-call | tf_op jit(solution)/shard_map/pallas_call | solution.py:545
  42.8 0.0 copy-start.1
  42.8 2.0 %copy.34 = f32[35,9,512]{2,0,1:T(8,128)} copy(f32[35,9,512]{2,0,1:T(8,128)} %bitcast.17) | data formatting | bytes 1290240
  44.9 0.0 copy-done.1
  44.9 0.6 %copy.35 = f32[3,16]{1,0:T(4,128)} copy(f32[3,16]{1,0:T(4,128)S(1)} %copy-done.1) | data formatting | bytes 384
  (5 shorter events, 0.1 us)
Async XLA Ops:
  0.6 5.5 %copy-start = (bf16[2,35,9,512]{3,0,2,1:T(2,128)(2,1)S(1)}, bf16[2,35,9,512]{3,0,2,1:T(2,128)(2,1)}, u32[]{:S(2)}) copy-start(bf16[2,35,9,512]{3,0,2,1:T(2,128)(2,1)} %param.16) | copy-start | bytes 1935364
  42.8 2.0 %copy-start.1 = (f32[3,16]{1,0:T(4,128)S(1)}, f32[3,16]{1,0:T(4,128)}, u32[]{:S(2)}) copy-start(f32[3,16]{1,0:T(4,128)} %get-tuple-element.13) | copy-start | bytes 580

commit v2 on v1

--- a/solution.py
+++ b/solution.py
@@ -40,14 +40,19 @@
     jac_ref,
     ang_ref,
     scale_ref,
-    amat_ref,
-    lmat_ref,
+    stiff_ref,
+    face_ref,
     nbr_ref,
     nface_ref,
     send_ref,
+    sface_ref,
     cell_ref,
     out_ref,
     hist_ref,
+    amat_ref,
+    lmat_ref,
+    square,
+    send_row,
     q_buf,
     p_buf,
     b_buf,
@@ -134,6 +139,28 @@
 
     lax.fori_loop(0, per_dev, greet, 0)
 
+    three_zero = jnp.zeros((128, 256), F32)
+
+    def three_parts(matrix, step_lanes, rows):
+        square[0, 0:rows, 0:128] = matrix[0:rows]
+        high, low = split(square[0, 0:rows, :])
+        high, low = high.astype(F32), low.astype(F32)
+        joined = high + pltpu.roll(high, step_lanes, 1) + pltpu.roll(low, 2 * step_lanes, 1)
+        return joined.astype(BF16)
+
+    square[0] = three_zero
+    for d in range(3):
+        square[1] = three_zero
+        square[1, 0:basis, 0:basis] = stiff_ref[d]
+        flipped = square[1, :, 0:128].T
+        amat_ref[d * ROWS : (d + 1) * ROWS, :] = three_parts(flipped, KROWS, ROWS)
+    square[1] = three_zero
+    for g in range(4):
+        square[1, g * 16 : g * 16 + face_ref.shape[0], 0:basis] = face_ref[:, g, :]
+    tracing = square[1, :, 0:128]
+    amat_ref[3 * ROWS : 3 * ROWS + 64, :] = three_parts(tracing, KROWS, 64)
+    lmat_ref[...] = three_parts(tracing.T, 64, ROWS)
+
     p_speed, s_speed, density = p_ref[...], s_ref[...], rho_ref[...]
     lame = density * (p_speed * p_speed - 2.0 * s_speed * s_speed)
     shear = density * s_speed * s_speed
@@ -176,10 +203,20 @@
             onehot[block * 256 : (block + 1) * 256, f * count : (f + 1) * count] = jnp.where(
                 hit, 1.0, 0.0
             ).astype(BF16)
-    send_ids = lax.broadcasted_iota(jnp.int32, (256, ghosts), 0)
-    for block in range(locals_all // 256):
-        hit = (send_ids + block * 256) == send_ref[...]
-        send_hot[block * 256 : (block + 1) * 256, :] = jnp.where(hit, 1.0, 0.0).astype(BF16)
+    send_row[...] = jnp.zeros_like(send_row)
+    send_row[0:4, 0:64] = sface_ref[...] * count + send_ref[...]
+    send_lane = lax.broadcasted_iota(jnp.int32, (8, 128), 1)
+    shifted = pltpu.roll(send_row[...], 64, 1)
+    send_ids = lax.broadcasted_iota(jnp.int32, (256, 128), 0)
+    for tile in range(2):
+        index = jnp.where(
+            send_lane[0:1] < 64, send_row[2 * tile : 2 * tile + 1, :], shifted[2 * tile + 1 : 2 * tile + 2]
+        )
+        for block in range(locals_all // 256):
+            hit = (send_ids + block * 256) == index
+            send_hot[block * 256 : (block + 1) * 256, tile * 128 : (tile + 1) * 128] = jnp.where(
+                hit, 1.0, 0.0
+            ).astype(BF16)
 
     q_buf[:, 32:ROWS, :] = jnp.zeros((9, 8, count), F32)
     f_buf[:, 32:ROWS, :] = jnp.zeros((9, 8, count), F32)
@@ -187,19 +224,23 @@
     b_buf[...] = jnp.zeros_like(b_buf)
     sums[...] = jnp.zeros_like(sums)
 
-    def load_operand(source):
+    half = count // 2
+    halves = (slice(0, half), slice(half, count))
+
+    def load_operand(source, h):
         for field in range(9):
-            high, low = split(source[field])
-            b_buf[field, 0:ROWS, :] = high
-            b_buf[field, KROWS : KROWS + ROWS, :] = low
-            b_buf[field, 2 * KROWS : 2 * KROWS + ROWS, :] = high
-
-    def volume(rows):
-        for field in range(9):
-            y_buf[field, 0:rows, :] = wide_dot(amat_ref[0:rows, :], b_buf[field])
-
-    def advance(factor):
-        for t in range(tiles):
+            high, low = split(source[field, :, halves[h]])
+            b_buf[field, 0:ROWS, halves[h]] = high
+            b_buf[field, KROWS : KROWS + ROWS, halves[h]] = low
+            b_buf[field, 2 * KROWS : 2 * KROWS + ROWS, halves[h]] = high
+
+    def volume(field, h, start=0, stop=3 * ROWS):
+        y_buf[field, start:stop, halves[h]] = wide_dot(
+            amat_ref[start:stop, 0 : 3 * KROWS], b_buf[field, :, halves[h]]
+        )
+
+    def advance(factor, h):
+        for t in range(h * tiles // 2, (h + 1) * tiles // 2):
             lanes = slice(t * 128, (t + 1) * 128)
             lame_c = coef[18, :, lanes] * factor
             two_c = coef[19, :, lanes] * factor
@@ -234,6 +275,7 @@
                             term = coef[9 + d * 3 + a, :, lanes] * stress[picks[a]][d]
                             total = term if total is None else total + term
                     p_buf[6 + b, rows, lanes] = q_buf[6 + b, rows, lanes] - factor * total
+                yield
 
     def element_sums(step):
         for field in range(9):
@@ -256,6 +298,7 @@
             sums[0, :, lanes] += first
             sums[1, :, lanes] += second
             sums[2, :, lanes] += third
+            yield
 
     def ghost_copy(step, link):
         slot, tile, to_ok, target, from_ok, source = link
@@ -273,19 +316,100 @@
         sum(link[2].astype(jnp.int32) for link in links) + target_count(me, n_dev, per_dev),
     )
 
+    def cell_copy(c, cell, dst, sem):
+        target = lax.rem(cell, n_dev)
+        slot = lax.div(cell, n_dev)
+        return pltpu.make_async_remote_copy(
+            src_ref=cells_out,
+            dst_ref=dst.at[slot],
+            send_sem=h_send.at[c],
+            recv_sem=sem.at[slot],
+            device_id=place(target),
+            device_id_type=MESH,
+        )
+
+    def to_cell(c, cell, dst, sem):
+        target = lax.rem(cell, n_dev)
+        slot = lax.div(cell, n_dev)
+
+        @pl.when(target != me)
+        def _():
+            cell_copy(c, cell, dst, sem).start()
+
+        @pl.when(target == me)
+        def _():
+            dst[slot] = cells_out[...]
+
+    low_cell = per_dev * me - 1
+    high_cell = per_dev * me + per_dev
+
+    def send_cells():
+        parts = [jnp.sum(sums[k], axis=0, keepdims=True) for k in range(3)]
+        first, second, third = parts
+        gain = KERNEL_WEIGHT * FULL
+        speed_sq = s_speed * s_speed
+        terms = [
+            gain * (2.0 * density * p_speed * first),
+            gain * (density * s_speed * (2.0 * second - 4.0 * first)),
+            gain * ((p_speed * p_speed - 2.0 * speed_sq) * first + speed_sq * second + third),
+        ]
+        term_row = lax.broadcasted_iota(jnp.int32, (8, count), 0)
+        stacked = jnp.where(term_row == 0, terms[0], 0.0)
+        stacked = jnp.where(term_row == 1, terms[1], stacked)
+        stacked = jnp.where(term_row == 2, terms[2], stacked)
+        entry = cell_ref[...]
+        owner = lax.shift_right_logical(entry, per_dev.bit_length() - 1)
+        coarse = (entry - owner * per_dev) * n_dev + owner
+        relative = coarse - (per_dev * me - 1)
+        hot = jnp.where(
+            lax.broadcasted_iota(jnp.int32, (128, count), 0) == relative, 1.0, 0.0
+        ).astype(F32)
+        cells_out[...] = lax.dot_general(
+            stacked,
+            hot,
+            (((1,), (1,)), ((), ())),
+            precision=lax.Precision.HIGHEST,
+            preferred_element_type=F32,
+        )
+
+        def send_main(c, carry):
+            to_cell(c, per_dev * me + c, cells_main, h_recv_main)
+            return carry
+
+        lax.fori_loop(0, per_dev, send_main, 0)
+
+        @pl.when(me > 0)
+        def _():
+            to_cell(per_dev, low_cell, cells_side, h_recv_side)
+
+        @pl.when(me < n_dev - 1)
+        def _():
+            to_cell(per_dev + 1, high_cell, cells_side, h_recv_side)
+
     def step_body(step, carry):
-        load_operand(q_buf)
+        load_operand(q_buf, 0)
+        load_operand(q_buf, 1)
+        base = 3 * ROWS
+        for field in range(9):
+            volume(field, 0)
 
         def sweep(_, inner):
-            volume(3 * ROWS)
-            advance(1.0)
-            load_operand(p_buf)
+            for h in range(2):
+                pieces = advance(1.0, h)
+                for field in range(9):
+                    volume(field, 1 - h)
+                    next(pieces)
+                for _ in pieces:
+                    pass
+                load_operand(p_buf, h)
             return inner
 
         lax.fori_loop(0, PICARD, sweep, 0)
-        element_sums(step)
-        volume(3 * ROWS + 64)
-        base = 3 * ROWS
+        for field in range(9):
+            volume(field, 0, base, base + 64)
+            volume(field, 1, 0, base + 64)
+        for _ in element_sums(step):
+            pass
         for field in range(9):
             for g in range(4):
                 high, low = split(y_buf[field, base + g * 16 : base + g * 16 + 16, :])
@@ -302,11 +426,23 @@
             def _(link=link):
                 ghost_copy(step, link).start()
 
-        advance(2.0)
-        for f in range(4):
-            columns = slice(f * count, (f + 1) * count)
+        @pl.when(step == steps - 1)
+        def _():
+            send_cells()
+
+        def side_work():
+            yield from advance(2.0, 0)
+            yield from advance(2.0, 1)
+
+        work = side_work()
+        for c in range(8):
+            columns = slice(c * half, (c + 1) * half)
             got = wide_dot(left_buf[...], onehot[0:locals_all, columns])
             far_buf[:, columns] = got[0:TRACE] + got[TRACE:]
+            for _ in range(3):
+                next(work, None)
+        for _ in work:
+            pass
 
         for link in links:
 
@@ -363,7 +499,7 @@
             fx_buf[0:64, :] = high
             fx_buf[64:128, :] = low
             fx_buf[128:192, :] = high
-            q_buf[field] = p_buf[field] - wide_dot(lmat_ref[...], fx_buf[...])
+            q_buf[field] = p_buf[field] - wide_dot(lmat_ref[:, 0:192], fx_buf[...])
         for link in links:
 
             @pl.when(link[2])
@@ -374,75 +510,6 @@
 
     lax.fori_loop(0, steps, step_body, 0)
     out_ref[...] = q_buf[:, 0:basis, :]
-
-    parts = [jnp.sum(sums[k], axis=0, keepdims=True) for k in range(3)]
-    first, second, third = parts
-    gain = KERNEL_WEIGHT * FULL
-    square = s_speed * s_speed
-    terms = [
-        gain * (2.0 * density * p_speed * first),
-        gain * (density * s_speed * (2.0 * second - 4.0 * first)),
-        gain * ((p_speed * p_speed - 2.0 * square) * first + square * second + third),
-    ]
-    term_row = lax.broadcasted_iota(jnp.int32, (8, count), 0)
-    stacked = jnp.where(term_row == 0, terms[0], 0.0)
-    stacked = jnp.where(term_row == 1, terms[1], stacked)
-    stacked = jnp.where(term_row == 2, terms[2], stacked)
-    entry = cell_ref[...]
-    owner = lax.shift_right_logical(entry, per_dev.bit_length() - 1)
-    coarse = (entry - owner * per_dev) * n_dev + owner
-    relative = coarse - (per_dev * me - 1)
-    hot = jnp.where(
-        lax.broadcasted_iota(jnp.int32, (128, count), 0) == relative, 1.0, 0.0
-    ).astype(F32)
-    cells_out[...] = lax.dot_general(
-        stacked,
-        hot,
-        (((1,), (1,)), ((), ())),
-        precision=lax.Precision.HIGHEST,
-        preferred_element_type=F32,
-    )
-
-    def cell_copy(c, cell, dst, sem):
-        target = lax.rem(cell, n_dev)
-        slot = lax.div(cell, n_dev)
-        return pltpu.make_async_remote_copy(
-            src_ref=cells_out,
-            dst_ref=dst.at[slot],
-            send_sem=h_send.at[c],
-            recv_sem=sem.at[slot],
-            device_id=place(target),
-            device_id_type=MESH,
-        )
-
-    def to_cell(c, cell, dst, sem):
-        target = lax.rem(cell, n_dev)
-        slot = lax.div(cell, n_dev)
-
-        @pl.when(target != me)
-        def _():
-            cell_copy(c, cell, dst, sem).start()
-
-        @pl.when(target == me)
-        def _():
-            dst[slot] = cells_out[...]
-
-    low_cell = per_dev * me - 1
-    high_cell = per_dev * me + per_dev
-
-    def send_main(c, carry):
-        to_cell(c, per_dev * me + c, cells_main, h_recv_main)
-        return carry
-
-    lax.fori_loop(0, per_dev, send_main, 0)
-
-    @pl.when(me > 0)
-    def _():
-        to_cell(per_dev, low_cell, cells_side, h_recv_side)
-
-    @pl.when(me < n_dev - 1)
-    def _():
-        to_cell(per_dev + 1, high_cell, cells_side, h_recv_side)
 
     def finish(j, carry):
         @pl.when(main_source(j) != me)
@@ -499,10 +566,9 @@
     return total + low.astype(jnp.int32) + high.astype(jnp.int32)
 
 
-def three_way(matrix):
-    high = lax.reduce_precision(matrix, 8, 7)
-    low = matrix - high
-    return jnp.concatenate([high, high, low], axis=1).astype(BF16)
+def hand_over(state_ref, cells_ref, out_ref, hist_ref):
+    out_ref[...] = state_ref[...]
+    hist_ref[...] = cells_ref[...]
 
 
 def shards(
@@ -526,20 +592,7 @@
 ):
     basis, fields, count = adjoint.shape
     steps = forward.shape[0]
-    modes = face_basis.shape[2]
     per_dev = count // 32
-    moving = jnp.pad(
-        jnp.transpose(stiffness, (0, 2, 1)), ((0, 0), (0, ROWS - basis), (0, KROWS - basis))
-    ).reshape(3 * ROWS, KROWS)
-    tracing = jnp.pad(
-        jnp.transpose(face_basis, (0, 2, 1)), ((0, 0), (0, 16 - modes), (0, KROWS - basis))
-    ).reshape(64, KROWS)
-    amat = three_way(jnp.concatenate([moving, tracing], axis=0))
-    lifting = jnp.pad(
-        jnp.transpose(face_basis, (1, 0, 2)), ((0, ROWS - basis), (0, 0), (0, 16 - modes))
-    ).reshape(ROWS, 64)
-    lmat = three_way(lifting)
-    send_index = (send_faces * count + send_elements).reshape(1, 256)
     row = lambda value: value.reshape(1, count)
     vmem = pl.BlockSpec(memory_space=pltpu.VMEM)
     state, kernels = pl.pallas_call(
@@ -548,9 +601,13 @@
             jax.ShapeDtypeStruct((fields, basis, count), F32),
             jax.ShapeDtypeStruct((3, per_dev), F32),
         ),
-        in_specs=[vmem] * 14,
+        in_specs=[vmem] * 15,
         out_specs=(vmem, vmem),
         scratch_shapes=[
+            pltpu.VMEM((3 * ROWS + 64, 256), BF16),
+            pltpu.VMEM((ROWS, 256), BF16),
+            pltpu.VMEM((2, 128, 256), F32),
+            pltpu.VMEM((8, 128), jnp.int32),
             pltpu.VMEM((9, ROWS, count), F32),
             pltpu.VMEM((9, ROWS, count), F32),
             pltpu.VMEM((9, 3 * KROWS, count), BF16),
@@ -577,7 +634,7 @@
             pltpu.SemaphoreType.DMA((per_dev,)),
         ],
         compiler_params=pltpu.CompilerParams(
-            collective_id=0, has_side_effects=True, vmem_limit_bytes=56 * 1024 * 1024
+            collective_id=0, has_side_effects=True, vmem_limit_bytes=36 * 1024 * 1024
         ),
     )(
         jnp.transpose(adjoint, (1, 0, 2)),
@@ -588,13 +645,23 @@
         inv_jacobian,
         face_angles,
         face_scale,
-        amat,
-        lmat,
+        stiffness,
+        jnp.transpose(face_basis, (2, 0, 1)),
         neighbours,
         neighbour_face,
-        send_index,
+        send_elements,
+        send_faces,
         row(cell_index),
     )
+    state, kernels = pl.pallas_call(
+        hand_over,
+        out_shape=(
+            jax.ShapeDtypeStruct(state.shape, F32),
+            jax.ShapeDtypeStruct(kernels.shape, F32),
+        ),
+        in_specs=[vmem] * 2,
+        out_specs=(vmem, vmem),
+    )(state, kernels)
     return jnp.transpose(state, (1, 0, 2)), kernels
 
 

time: 45.8 us -> 35.7 us (0.78)
  local copies, waits for them, and re-layouts: 6.73 us -> 2.76 us
  Pallas kernels: 35.8 us -> 31.9 us
  other arithmetic: 2.24 us -> 0 us
    pallas_call x1, Pallas kernels: 35.8 us -> 29.9 us  [shards(): pl.pallas_call(functools.partial(kernel, n_depth, n_map), out_shape=(jax....]
    unnamed x10 -> x33, local copies, waits for them, and re-layouts: 5.99 us -> 2.76 us
    pallas_call x0 -> x1, Pallas kernels: none -> 2.03 us  [shards(): pl.pallas_call(hand_over, out_shape=(jax.ShapeDtypeStruct(state.shape, F3...]
    concatenate x2 -> x0, other arithmetic: 1.44 us -> none  [three_way(): return jnp.concatenate([high, high, low], axis=1).astype(BF16)]
    add x1 -> x0, other arithmetic: 0.77 us -> none  [shards(): send_index = (send_faces * count + send_elements).reshape(1, 256)]
    reshape x2 -> x0, local copies, waits for them, and re-layouts: 0.71 us -> none  [the longest x1 0.64 us: shards(): send_index = (send_faces * count + send_elements).reshape(1, 256)]
where the time goes in v2:
time: 35.7 us; the launch traced here: 35.6 us
  Pallas kernels  31.9 us (89%)
  local copies, waits for them, and re-layouts  2.76 us (8%)
  between operations  0.88 us (2%)
    pallas_call x1, Pallas kernels, shards(): pl.pallas_call(functools.partial(kernel, n_depth, n_map), out_shape=(jax....  29.9 us
    unnamed x33, local copies, waits for them, and re-layouts  2.76 us
    pallas_call x1, Pallas kernels, shards(): pl.pallas_call(hand_over, out_shape=(jax.ShapeDtypeStruct(state.shape, F3...  2.03 us

profile of v2, /device:TPU:0, one launch (start us, length us, event | category | flops | bytes accessed | tf_op | source)
XLA Modules:
  0.0 35.6 jit_solution(9647450481743361674)
XLA Ops:
  0.6 0.0 copy-start
  0.6 0.0 copy-start.2
  0.7 0.0 copy-start.3
  0.7 0.0 copy-start.4
  0.7 0.0 copy-start.5
  0.8 1.2 %copy.19 = bf16[2,35,9,512]{3,1,2,0:T(8,128)(2,1)S(1)} copy(bf16[2,35,9,512]{3,0,2,1:T(2,128)(2,1)} %param.16) | data formatting | bytes 1290240 | tf_op args[1]
  2.0 0.0 copy-done
  2.0 0.0 copy-done.2
  2.0 0.0 copy-done.3
  2.0 0.0 copy-done.4
  2.0 0.0 copy-done.5
  2.1 0.0 copy-done.6
  2.1 0.0 copy-done.7
  2.1 0.0 copy-done.8
  2.1 0.0 copy-done.9
  2.1 0.0 copy-done.10
  2.1 0.0 copy-done.11
  2.1 0.0 copy-done.12
  2.1 0.0 copy-done.13
  2.1 0.0 copy-done.14
  2.1 29.9 %shard_map.158 = (f32[9,35,512]{2,1,0:T(8,128)S(1)}, f32[3,16]{1,0:T(4,128)S(1)}) custom-call(f32[9,35,512]{2,1,0:T(8,128)S(1)} %bitcast.11, bf16[2,9,35,512]{3,2,1,0:T(8,128)(2,1)S(1)} %bitcast.10, f32[1,512]{1,0:T(1,128)S(1)} %bitcast.13, f32[1,512]{1,0:T(1,128)S(1)} %bitcast.14, f32[1,512]{1,0:T(1,128)S(1)} %bitcast.15, f32[3,3,512]{2,1,0:T(4,128)S(1)} %copy-done.4, ...), custom_call_target="tpu_custom_call" | custom-call | tf_op jit(solution)/shard_map/pallas_call | solution.py:598
  32.1 0.9 %copy-done.1 = f32[9,35,512]{2,1,0:T(8,128)} copy-done((f32[9,35,512]{2,1,0:T(8,128)}, f32[9,35,512]{2,1,0:T(8,128)S(1)}, u32[]{:S(2)}) %copy-start.1) | copy-done | bytes 645144
  33.0 0.6 %copy-done.15 = f32[3,16]{1,0:T(4,128)} copy-done((f32[3,16]{1,0:T(4,128)}, f32[3,16]{1,0:T(4,128)S(1)}, u32[]{:S(2)}) %copy-start.15) | copy-done | bytes 216
  33.5 2.0 %shard_map.159 = (f32[9,35,512]{2,1,0:T(8,128)}, f32[3,16]{1,0:T(4,128)}) custom-call(f32[9,35,512]{2,1,0:T(8,128)} %copy-done.1, f32[3,16]{1,0:T(4,128)} %copy-done.15), custom_call_target="tpu_custom_call" | custom-call | tf_op jit(solution)/shard_map/pallas_call | solution.py:656
  (11 shorter events, 0.0 us)
Async XLA Ops:
  0.6 1.4 %copy-start = (f32[35,9,512]{2,0,1:T(8,128)S(1)}, f32[35,9,512]{2,0,1:T(8,128)}, u32[]{:S(2)}) copy-start(f32[35,9,512]{2,0,1:T(8,128)} %param.15) | copy-start | bytes 1935364
  0.6 1.4 %copy-start.2 = (f32[3,35,35]{2,1,0:T(8,128)S(1)}, f32[3,35,35]{2,1,0:T(8,128)}, u32[]{:S(2)}) copy-start(f32[3,35,35]{2,1,0:T(8,128)} %stiff_ref.1) | copy-start | bytes 44104
  0.7 1.4 %copy-start.3 = (f32[4,35,15]{1,0,2:T(4,128)S(1)}, f32[4,35,15]{1,0,2:T(4,128)}, u32[]{:S(2)}) copy-start(f32[4,35,15]{1,0,2:T(4,128)} %param.24) | copy-start | bytes 25204
  0.7 1.4 %copy-start.4 = (f32[3,3,512]{2,1,0:T(4,128)S(1)}, f32[3,3,512]{2,1,0:T(4,128)}, u32[]{:S(2)}) copy-start(f32[3,3,512]{2,1,0:T(4,128)} %jac_ref.1) | copy-start | bytes 55300
  0.7 1.4 %copy-start.5 = (f32[2,4,512]{2,1,0:T(4,128)S(1)}, f32[2,4,512]{2,1,0:T(4,128)}, u32[]{:S(2)}) copy-start(f32[2,4,512]{2,1,0:T(4,128)} %ang_ref.1) | copy-start | bytes 49156
  0.7 1.4 %copy-start.6 = (f32[4,512]{1,0:T(4,128)S(1)}, f32[4,512]{1,0:T(4,128)}, u32[]{:S(2)}) copy-start(f32[4,512]{1,0:T(4,128)} %scale_ref.1) | copy-start | bytes 24580
  0.7 1.4 %copy-start.7 = (s32[4,512]{1,0:T(4,128)S(1)}, s32[4,512]{1,0:T(4,128)}, u32[]{:S(2)}) copy-start(s32[4,512]{1,0:T(4,128)} %nbr_ref.1) | copy-start | bytes 24580
  0.7 1.4 %copy-start.8 = (s32[4,512]{1,0:T(4,128)S(1)}, s32[4,512]{1,0:T(4,128)}, u32[]{:S(2)}) copy-start(s32[4,512]{1,0:T(4,128)} %nface_ref.1) | copy-start | bytes 24580
  0.7 1.4 %copy-start.9 = (f32[512]{0:T(512)S(1)}, f32[512]{0:T(512)}, u32[]{:S(2)}) copy-start(f32[512]{0:T(512)} %param.17) | copy-start | bytes 6148
  0.7 1.4 %copy-start.10 = (f32[512]{0:T(512)S(1)}, f32[512]{0:T(512)}, u32[]{:S(2)}) copy-start(f32[512]{0:T(512)} %param.18) | copy-start | bytes 6148
  0.7 1.4 %copy-start.11 = (f32[512]{0:T(512)S(1)}, f32[512]{0:T(512)}, u32[]{:S(2)}) copy-start(f32[512]{0:T(512)} %param.19) | copy-start | bytes 6148
  0.7 1.4 %copy-start.12 = (s32[4,64]{1,0:T(4,128)S(1)}, s32[4,64]{1,0:T(4,128)}, u32[]{:S(2)}) copy-start(s32[4,64]{1,0:T(4,128)} %send_ref.1) | copy-start | bytes 3076
  0.8 1.4 %copy-start.13 = (s32[4,64]{1,0:T(4,128)S(1)}, s32[4,64]{1,0:T(4,128)}, u32[]{:S(2)}) copy-start(s32[4,64]{1,0:T(4,128)} %sface_ref.1) | copy-start | bytes 3076
  0.8 1.4 %copy-start.14 = (s32[512]{0:T(512)S(1)}, s32[512]{0:T(512)}, u32[]{:S(2)}) copy-start(s32[512]{0:T(512)} %param.29) | copy-start | bytes 6148
  32.0 0.9 %copy-start.1 = (f32[9,35,512]{2,1,0:T(8,128)}, f32[9,35,512]{2,1,0:T(8,128)S(1)}, u32[]{:S(2)}) copy-start(f32[9,35,512]{2,1,0:T(8,128)S(1)} %get-tuple-element.6.state_ref) | copy-start | bytes 1935364
  32.9 0.6 %copy-start.15 = (f32[3,16]{1,0:T(4,128)}, f32[3,16]{1,0:T(4,128)S(1)}, u32[]{:S(2)}) copy-start(f32[3,16]{1,0:T(4,128)S(1)} %get-tuple-element.7.cells_ref) | copy-start | bytes 580

commit v3 on v2

--- a/solution.py
+++ b/solution.py
@@ -303,7 +303,7 @@
     def ghost_copy(step, link):
         slot, tile, to_ok, target, from_ok, source = link
         return pltpu.make_async_remote_copy(
-            src_ref=send_buf.at[step, tile],
+            src_ref=send_buf.at[step, slot],
             dst_ref=recv_buf.at[step, slot],
             send_sem=g_send.at[step, slot],
             recv_sem=g_recv.at[step, slot],
@@ -390,6 +390,7 @@
         load_operand(q_buf, 0)
         load_operand(q_buf, 1)
         base = 3 * ROWS
+        half_lane = lax.broadcasted_iota(jnp.int32, (TRACE // 2, 128), 1)
         for field in range(9):
             volume(field, 0)
 
@@ -419,7 +420,11 @@
         picked = wide_dot(left_buf[...], send_hot[...])
         picked = picked[0:TRACE] + picked[TRACE:]
         for tile in range(2):
-            send_buf[step, tile] = picked[:, tile * 128 : (tile + 1) * 128]
+            block = picked[:, tile * 128 : (tile + 1) * 128]
+            top, bottom = block[0 : TRACE // 2], block[TRACE // 2 :]
+            turned_top, turned_bottom = pltpu.roll(top, 64, 1), pltpu.roll(bottom, 64, 1)
+            send_buf[step, 2 * tile] = jnp.where(half_lane < 64, top, turned_bottom)
+            send_buf[step, 2 * tile + 1] = jnp.where(half_lane < 64, turned_top, bottom)
         for link in links:
 
             @pl.when(link[2])
@@ -450,10 +455,11 @@
             def _(link=link):
                 ghost_copy(step, link).wait_recv()
 
-        lane = lax.broadcasted_iota(jnp.int32, (TRACE, 128), 1)
         for tile in range(2):
-            both = jnp.where(lane < 64, recv_buf[step, 2 * tile], recv_buf[step, 2 * tile + 1])
-            high, low = split(both)
+            even, odd = recv_buf[step, 2 * tile], recv_buf[step, 2 * tile + 1]
+            top = jnp.where(half_lane < 64, even, pltpu.roll(odd, 64, 1))
+            bottom = jnp.where(half_lane < 64, pltpu.roll(even, 64, 1), odd)
+            high, low = split(jnp.concatenate([top, bottom], axis=0))
             ghost_left[0:TRACE, tile * 128 : (tile + 1) * 128] = high
             ghost_left[TRACE:, tile * 128 : (tile + 1) * 128] = low
         for f in range(4):
@@ -566,9 +572,15 @@
     return total + low.astype(jnp.int32) + high.astype(jnp.int32)
 
 
-def hand_over(state_ref, cells_ref, out_ref, hist_ref):
-    out_ref[...] = state_ref[...]
-    hist_ref[...] = cells_ref[...]
+def hand_over(state_ref, cells_ref, out_ref, hist_ref, sems):
+    copies = [
+        pltpu.make_async_copy(state_ref, out_ref, sems.at[0]),
+        pltpu.make_async_copy(cells_ref, hist_ref, sems.at[1]),
+    ]
+    for copy in copies:
+        copy.start()
+    for copy in copies:
+        copy.wait()
 
 
 def shards(
@@ -595,6 +607,7 @@
     per_dev = count // 32
     row = lambda value: value.reshape(1, count)
     vmem = pl.BlockSpec(memory_space=pltpu.VMEM)
+    anywhere = pl.BlockSpec(memory_space=pl.ANY)
     state, kernels = pl.pallas_call(
         functools.partial(kernel, n_depth, n_map),
         out_shape=(
@@ -622,8 +635,8 @@
             pltpu.VMEM((9, 64, count), F32),
             pltpu.VMEM((192, count), BF16),
             pltpu.VMEM((3, 8, count), F32),
-            pltpu.VMEM((steps, 2, TRACE, 128), F32),
-            pltpu.VMEM((steps, 4, TRACE, 128), F32),
+            pltpu.VMEM((steps, 4, TRACE // 2, 128), F32),
+            pltpu.VMEM((steps, 4, TRACE // 2, 128), F32),
             pltpu.VMEM((8, 128), F32),
             pltpu.VMEM((per_dev, 8, 128), F32),
             pltpu.VMEM((per_dev, 8, 128), F32),
@@ -659,8 +672,10 @@
             jax.ShapeDtypeStruct(state.shape, F32),
             jax.ShapeDtypeStruct(kernels.shape, F32),
         ),
-        in_specs=[vmem] * 2,
-        out_specs=(vmem, vmem),
+        in_specs=[anywhere] * 2,
+        out_specs=(anywhere, anywhere),
+        scratch_shapes=[pltpu.SemaphoreType.DMA((2,))],
+        compiler_params=pltpu.CompilerParams(vmem_limit_bytes=1024 * 1024),
     )(state, kernels)
     return jnp.transpose(state, (1, 0, 2)), kernels
 

time: 35.7 us -> 31.2 us (0.87)
  Pallas kernels: 31.9 us -> 28.9 us
  local copies, waits for them, and re-layouts: 2.76 us -> 1.29 us
    pallas_call x1, Pallas kernels: 29.9 us -> 28 us  [shards(): pl.pallas_call(functools.partial(kernel, n_depth, n_map), out_shape=(jax....]
    unnamed x33 -> x29, local copies, waits for them, and re-layouts: 2.76 us -> 1.29 us
    pallas_call x1, Pallas kernels: 2.03 us -> 0.88 us  [shards(): pl.pallas_call(hand_over, out_shape=(jax.ShapeDtypeStruct(state.shape, F3...]
where the time goes in v3:
time: 31.2 us; the launch traced here: 31 us
  Pallas kernels  28.9 us (93%)
  local copies, waits for them, and re-layouts  1.29 us (4%)
  between operations  0.87 us (3%)
    pallas_call x1, Pallas kernels, shards(): pl.pallas_call(functools.partial(kernel, n_depth, n_map), out_shape=(jax....  28 us
    unnamed x29, local copies, waits for them, and re-layouts  1.29 us
    pallas_call x1, Pallas kernels, shards(): pl.pallas_call(hand_over, out_shape=(jax.ShapeDtypeStruct(state.shape, F3...  0.88 us

profile of v3, /device:TPU:0, one launch (start us, length us, event | category | flops | bytes accessed | tf_op | source)
XLA Modules:
  0.0 31.0 jit_solution(5760092813659038154)
XLA Ops:
  0.6 0.0 copy-start
  0.6 0.0 copy-start.1
  0.7 0.0 copy-start.2
  0.7 0.0 copy-start.3
  0.7 0.0 copy-start.4
  0.7 0.0 copy-start.5
  0.7 0.0 copy-start.6
  0.7 0.0 copy-start.7
  0.7 0.0 copy-start.8
  0.7 0.0 copy-start.9
  0.7 0.0 copy-start.10
  0.7 0.0 copy-start.11
  0.8 0.0 copy-start.12
  0.8 0.0 copy-start.13
  0.8 1.2 %copy.19 = bf16[2,35,9,512]{3,1,2,0:T(8,128)(2,1)S(1)} copy(bf16[2,35,9,512]{3,0,2,1:T(2,128)(2,1)} %param.16) | data formatting | bytes 1290240 | tf_op args[1]
  2.0 0.0 copy-done
  2.0 0.0 copy-done.1
  2.0 0.0 copy-done.2
  2.0 0.0 copy-done.3
  2.0 0.0 copy-done.4
  2.1 0.0 copy-done.5
  2.1 0.0 copy-done.6
  2.1 28.0 %shard_map.158 = (f32[9,35,512]{2,1,0:T(8,128)S(1)}, f32[3,16]{1,0:T(4,128)S(1)}) custom-call(f32[9,35,512]{2,1,0:T(8,128)S(1)} %bitcast.11, bf16[2,9,35,512]{3,2,1,0:T(8,128)(2,1)S(1)} %bitcast.10, f32[1,512]{1,0:T(1,128)S(1)} %bitcast.13, f32[1,512]{1,0:T(1,128)S(1)} %bitcast.14, f32[1,512]{1,0:T(1,128)S(1)} %bitcast.15, f32[3,3,512]{2,1,0:T(4,128)S(1)} %copy-done.3, ...), custom_call_target="tpu_custom_call" | custom-call | tf_op jit(solution)/shard_map/pallas_call | solution.py:611
  30.1 0.9 %shard_map.159 = (f32[9,35,512]{2,1,0:T(8,128)}, f32[3,16]{1,0:T(4,128)}) custom-call(f32[9,35,512]{2,1,0:T(8,128)S(1)} %get-tuple-element.6.state_ref, f32[3,16]{1,0:T(4,128)S(1)} %get-tuple-element.7.cells_ref), custom_call_target="tpu_custom_call" | custom-call | tf_op jit(solution)/shard_map/pallas_call | solution.py:669
  (7 shorter events, 0.0 us)
Async XLA Ops:
  0.6 1.4 %copy-start = (f32[35,9,512]{2,0,1:T(8,128)S(1)}, f32[35,9,512]{2,0,1:T(8,128)}, u32[]{:S(2)}) copy-start(f32[35,9,512]{2,0,1:T(8,128)} %param.15) | copy-start | bytes 1935364
  0.6 1.4 %copy-start.1 = (f32[3,35,35]{2,1,0:T(8,128)S(1)}, f32[3,35,35]{2,1,0:T(8,128)}, u32[]{:S(2)}) copy-start(f32[3,35,35]{2,1,0:T(8,128)} %stiff_ref.1) | copy-start | bytes 44104
  0.7 1.4 %copy-start.2 = (f32[4,35,15]{1,0,2:T(4,128)S(1)}, f32[4,35,15]{1,0,2:T(4,128)}, u32[]{:S(2)}) copy-start(f32[4,35,15]{1,0,2:T(4,128)} %param.24) | copy-start | bytes 25204
  0.7 1.4 %copy-start.3 = (f32[3,3,512]{2,1,0:T(4,128)S(1)}, f32[3,3,512]{2,1,0:T(4,128)}, u32[]{:S(2)}) copy-start(f32[3,3,512]{2,1,0:T(4,128)} %jac_ref.1) | copy-start | bytes 55300
  0.7 1.4 %copy-start.4 = (f32[2,4,512]{2,1,0:T(4,128)S(1)}, f32[2,4,512]{2,1,0:T(4,128)}, u32[]{:S(2)}) copy-start(f32[2,4,512]{2,1,0:T(4,128)} %ang_ref.1) | copy-start | bytes 49156
  0.7 1.4 %copy-start.5 = (f32[4,512]{1,0:T(4,128)S(1)}, f32[4,512]{1,0:T(4,128)}, u32[]{:S(2)}) copy-start(f32[4,512]{1,0:T(4,128)} %scale_ref.1) | copy-start | bytes 24580
  0.7 1.4 %copy-start.6 = (s32[4,512]{1,0:T(4,128)S(1)}, s32[4,512]{1,0:T(4,128)}, u32[]{:S(2)}) copy-start(s32[4,512]{1,0:T(4,128)} %nbr_ref.1) | copy-start | bytes 24580
  0.7 1.4 %copy-start.7 = (s32[4,512]{1,0:T(4,128)S(1)}, s32[4,512]{1,0:T(4,128)}, u32[]{:S(2)}) copy-start(s32[4,512]{1,0:T(4,128)} %nface_ref.1) | copy-start | bytes 24580
  0.7 1.4 %copy-start.8 = (f32[512]{0:T(512)S(1)}, f32[512]{0:T(512)}, u32[]{:S(2)}) copy-start(f32[512]{0:T(512)} %param.17) | copy-start | bytes 6148
  0.7 1.4 %copy-start.9 = (f32[512]{0:T(512)S(1)}, f32[512]{0:T(512)}, u32[]{:S(2)}) copy-start(f32[512]{0:T(512)} %param.18) | copy-start | bytes 6148
  0.7 1.4 %copy-start.10 = (f32[512]{0:T(512)S(1)}, f32[512]{0:T(512)}, u32[]{:S(2)}) copy-start(f32[512]{0:T(512)} %param.19) | copy-start | bytes 6148
  0.7 1.4 %copy-start.11 = (s32[4,64]{1,0:T(4,128)S(1)}, s32[4,64]{1,0:T(4,128)}, u32[]{:S(2)}) copy-start(s32[4,64]{1,0:T(4,128)} %send_ref.1) | copy-start | bytes 3076
  0.8 1.4 %copy-start.12 = (s32[4,64]{1,0:T(4,128)S(1)}, s32[4,64]{1,0:T(4,128)}, u32[]{:S(2)}) copy-start(s32[4,64]{1,0:T(4,128)} %sface_ref.1) | copy-start | bytes 3076
  0.8 1.4 %copy-start.13 = (s32[512]{0:T(512)S(1)}, s32[512]{0:T(512)}, u32[]{:S(2)}) copy-start(s32[512]{0:T(512)} %param.29) | copy-start | bytes 6148
